TPU v7x, 512 devices: a whole 4x8x8 slice. The times are simulated.
512 devices in a mesh: row: 16 (over x_hi, z), col: 32 (over y, x_lo, core).
Axes of the slice: x: 4 (x_hi: 2, x_lo: 2; x = x_hi * 2 + x_lo), y: 8, z: 8, core: 2. Of those that a mesh axis runs over, the one named last changes fastest.
Arguments:
- activations: bfloat16 [1024, 28672], P('row', 'col'), may hold values from -0.1875 to 0.1875
- cotangent: bfloat16 [1024, 16384], P('col', 'row'), may hold values from -6 to 6
- down_weight: bfloat16 [28672, 16384], P('col', 'row'), may hold values from -0.046875 to 0.046875
- row_order: int32 [1024], replicated, may hold values from 0 to 1023, each once
Outputs:
- weight_grad: bfloat16 [28672, 16384], P('col', 'row')
- input_grad: bfloat16 [1024, 28672], P('row', 'col')
Inputs may be any that keep to these rules, and one draw needn't show every extreme that they name: `row_order`: each of the 1024 rows is named exactly once.
All inputs are finite; a program needn't handle non-finite values.
Results may differ from a plain program's by a relative error of at most 0.001.
Values may be sent and summed in bfloat16 or wider, within the bound.
A program may use at most 64 MiB of HBM per device.

v0:
```python
import jax
import jax.numpy as jnp
from jax import lax
from jax.sharding import PartitionSpec as P


def contract_rows(left, right):
    return lax.dot_general(
        left, right, (((0,), (0,)), ((), ())), preferred_element_type=jnp.float32
    )


def contract_cols(left, right):
    return lax.dot_general(
        left, right, (((1,), (1,)), ((), ())), preferred_element_type=jnp.float32
    )


def body(activations, cotangent, down_weight, row_order):
    gathered = lax.all_gather(cotangent, "col", axis=0, tiled=True)
    aligned = jnp.take(gathered, row_order, axis=0)
    all_rows = lax.all_gather(activations, "row", axis=0, tiled=True)
    weight_total = contract_rows(all_rows, aligned)
    weight_grad = weight_total.astype(jnp.bfloat16)
    partial_sums = contract_cols(aligned, down_weight)
    summed = lax.psum_scatter(partial_sums, "row", scatter_dimension=0, tiled=True)
    input_grad = summed.astype(jnp.bfloat16)
    return (weight_grad, input_grad)


def solution(mesh):
    in_specs = (P("row", "col"), P("col", "row"), P("col", "row"), P())
    out_specs = (P("col", "row"), P("row", "col"))
    return jax.shard_map(body, mesh=mesh, in_specs=in_specs, out_specs=out_specs, check_vma=False)
```

profile of v0, /device:TPU:8, one launch (start us, length us, event | category | flops | bytes accessed | tf_op | source)
XLA Modules:
  0.0 402.1 jit_solution(9003948174916197972)
XLA Ops:
  7.2 0.0 copy-start
  7.2 0.0 all-gather.3.cloned.1.call-start
  7.2 0.7 all-gather.3.cloned.1.call-update
  7.9 0.0 all-gather.5.cloned.1.call-start
  8.0 0.7 all-gather.5.cloned.1.call-update
  8.7 0.0 reduce-scatter.2.cloned.1.call-start
  8.7 0.7 compare_and_fusion
  9.4 0.7 fusion.1
  10.1 71.0 %all-gather.3.cloned.1.call-done = bf16[1024,1024]{1,0:T(8,128)(2,1)} async-done(((bf16[32,1024]{1,0:T(8,128)(2,1)}), bf16[1024,1024]{1,0:T(8,128)(2,1)}) %all-gather.3.cloned.1.call-update) | async-done | bytes 2097168 | tf_op jit(solution)/shard_map/all_gather | solution.py:20
  81.1 7.9 %gather_fusion = bf16[1024,1024]{1,0:T(8,128)(2,1)} fusion(bf16[1024,1024]{1,0:T(8,128)(2,1)} %all-gather.3.cloned.1.call-done, s32[1024]{0:T(1024)S(1)} %fusion.1), kind=kCustom, calls=%fused_computation | custom fusion | bytes 4198400 | tf_op jit(solution)/shard_map/jit(_take)/gather | solution.py:21
  89.0 0.0 copy-done
  89.0 5.8 %fusion = f32[1024,896]{1,0:T(8,128)} fusion(bf16[896,1024]{1,0:T(8,128)(2,1)S(1)} %copy-done, bf16[1024,1024]{1,0:T(8,128)(2,1)} %gather_fusion, pred[1024]{0:T(1024)(128)(4,1)S(1)} %compare_and_fusion), kind=kOutput, calls=%fused_computation.3 | convolution fusion | flops 1880096768 | bytes 7603200 | tf_op jit(solution)/shard_map/dot_general | solution.py:14
  94.7 0.0 reduce-scatter.2.cloned.1.call-update
  94.8 80.2 %all-gather.5.cloned.1.call-done = bf16[1024,896]{1,0:T(8,128)(2,1)} async-done(((bf16[64,896]{1,0:T(8,128)(2,1)}), bf16[1024,896]{1,0:T(8,128)(2,1)}) %all-gather.5.cloned.1.call-update) | async-done | bytes 1835024 | tf_op jit(solution)/shard_map/all_gather | solution.py:22
  175.0 5.9 %convert_bitcast_fusion = bf16[896,1024]{0,1:T(8,128)(2,1)} fusion(bf16[1024,896]{1,0:T(8,128)(2,1)} %all-gather.5.cloned.1.call-done, bf16[1024,1024]{1,0:T(8,128)(2,1)} %gather_fusion, pred[1024]{0:T(1024)(128)(4,1)S(1)} %compare_and_fusion), kind=kOutput, calls=%fused_computation.2 | convolution fusion | flops 1881014272 | bytes 5768192 | tf_op jit(solution)/shard_map/dot_general | solution.py:8
  180.9 3.8 copy.6
  184.7 209.3 %reduce-scatter.2.cloned.1.call-done = f32[64,896]{1,0:T(8,128)} async-done(((f32[1024,896]{1,0:T(8,128)}), f32[64,896]{1,0:T(8,128)}) %reduce-scatter.2.cloned.1.call-update) | async-done | bytes 229392 | tf_op jit(solution)/shard_map/reduce_scatter | solution.py:26
  394.0 1.6 convert_element_type.11
Async XLA Ops:
  7.2 81.8 %copy-start = (bf16[896,1024]{1,0:T(8,128)(2,1)S(1)}, bf16[896,1024]{1,0:T(8,128)(2,1)}, u32[]{:S(2)}) copy-start(bf16[896,1024]{1,0:T(8,128)(2,1)} %param.6) | copy-start | bytes 5505028
  7.2 73.9 %all-gather.3.cloned.1.call-start = ((), (), s32[]{:S(2)}) async-start(), calls=%async_computation.1 | async-start | bytes 2162688 | tf_op jit(solution)/shard_map/all_gather | solution.py:20
  7.9 167.1 %all-gather.5.cloned.1.call-start = ((), (), s32[]{:S(2)}) async-start(), calls=%async_computation.2 | async-start | bytes 1949696 | tf_op jit(solution)/shard_map/all_gather | solution.py:22
  8.7 385.3 %reduce-scatter.2.cloned.1.call-start = ((), (), s32[]{:S(2)}) async-start(), calls=%async_computation.3 | async-start | bytes 3899392 | tf_op jit(solution)/shard_map/reduce_scatter | solution.py:26
Sparse Core Ops, SparseCore 0:
  10.2 70.8 all-gather.2
  84.3 90.6 all-gather.4
  179.6 214.3 reduce-scatter.1
where the time goes:
time: 402 us
  waiting for transfers between devices  362 us (90%)
  between operations  13.8 us (3%)
  local copies, waits for them, and re-layouts  11.7 us (3%)
  matrix products  11.7 us (3%)
    reduce_scatter x1, waiting for transfers between devices, body(): lax.psum_scatter(partial_sums, 'row', scatter_dimension=0, tiled=True)  209 us
    all_gather x1, waiting for transfers between devices, body(): all_rows = lax.all_gather(activations, 'row', axis=0, tiled=True)  80.2 us
    all_gather x1, waiting for transfers between devices, body(): gathered = lax.all_gather(cotangent, 'col', axis=0, tiled=True)  71 us
  transfers between devices with their start and end apart: 3, of which 3 were waited for; matrix products, arithmetic and copies ran while one was open for 6% of the time, Pallas kernels for 0%

commit v1 on v0

--- a/solution.py
+++ b/solution.py
@@ -19,7 +19,8 @@
 def body(activations, cotangent, down_weight, row_order):
     gathered = lax.all_gather(cotangent, "col", axis=0, tiled=True)
     aligned = jnp.take(gathered, row_order, axis=0)
-    all_rows = lax.all_gather(activations, "row", axis=0, tiled=True)
+    repeated = jnp.stack([activations] * lax.axis_size("row"))
+    all_rows = jnp.concatenate(lax.all_to_all(repeated, "row", 0, 0), axis=0)
     weight_total = contract_rows(all_rows, aligned)
     weight_grad = weight_total.astype(jnp.bfloat16)
     partial_sums = contract_cols(aligned, down_weight)

time: 402 us -> 337 us (0.84)
  waiting for transfers between devices: 362 us -> 231 us
  blocking collectives: 0 us -> 66 us
    all_gather x1 -> x0, waiting for transfers between devices: 80.2 us -> none  [body(): all_rows = lax.all_gather(activations, 'row', axis=0, tiled=True)]
    all_to_all x0 -> x1, blocking collectives: none -> 66 us  [body(): all_rows = jnp.concatenate(lax.all_to_all(repeated, 'row', 0, 0), axis=0)]
    reduce_scatter x1, waiting for transfers between devices: 209 us -> 158 us  [body(): lax.psum_scatter(partial_sums, 'row', scatter_dimension=0, tiled=True)]
  transfers between devices with their start and end apart: 3 -> 2, of which waited for: 3 -> 2; matrix products, arithmetic and copies ran while one was open for 6% -> 3% of each run, Pallas kernels for 0% -> 0%
where the time goes in v1:
time: 337 us; the launch traced here: 336 us
  waiting for transfers between devices  231 us (69%)
  blocking collectives  66 us (20%)
  between operations  14.1 us (4%)
  local copies, waits for them, and re-layouts  12.8 us (4%)
  matrix products  9.55 us (3%)
    reduce_scatter x1, waiting for transfers between devices, body(): lax.psum_scatter(partial_sums, 'row', scatter_dimension=0, tiled=True)  158 us
    all_gather x1, waiting for transfers between devices, body(): gathered = lax.all_gather(cotangent, 'col', axis=0, tiled=True)  71.7 us
    all_to_all x1, blocking collectives, body(): all_rows = jnp.concatenate(lax.all_to_all(repeated, 'row', 0, 0), axis=0)  66 us
    gather x1, local copies, waits for them, and re-layouts, body(): aligned = jnp.take(gathered, row_order, axis=0)  7.91 us
  transfers between devices with their start and end apart: 2, of which 2 were waited for; matrix products, arithmetic and copies ran while one was open for 3% of the time, Pallas kernels for 0%

profile of v1, /device:TPU:8, one launch (start us, length us, event | category | flops | bytes accessed | tf_op | source)
XLA Modules:
  0.0 336.4 jit_solution(3002631359378489140)
XLA Ops:
  7.2 0.0 copy-start
  7.2 0.0 all-gather.2.cloned.1.call-start
  7.2 0.7 all-gather.2.cloned.1.call-update
  7.9 0.0 reduce-scatter.2.cloned.1.call-start
  8.0 0.7 compare_and_fusion
  8.7 0.7 fusion.1
  9.3 71.7 %all-gather.2.cloned.1.call-done = bf16[1024,1024]{1,0:T(8,128)(2,1)} async-done(((bf16[32,1024]{1,0:T(8,128)(2,1)}), bf16[1024,1024]{1,0:T(8,128)(2,1)}) %all-gather.2.cloned.1.call-update) | async-done | bytes 2097168 | tf_op jit(solution)/shard_map/all_gather | solution.py:20
  81.1 7.9 %gather_fusion = bf16[1024,1024]{1,0:T(8,128)(2,1)} fusion(bf16[1024,1024]{1,0:T(8,128)(2,1)} %all-gather.2.cloned.1.call-done, s32[1024]{0:T(1024)S(1)} %fusion.1), kind=kCustom, calls=%fused_computation | custom fusion | bytes 4198400 | tf_op jit(solution)/shard_map/jit(_take)/gather | solution.py:21
  89.0 0.0 copy-done
  89.0 5.8 %fusion = f32[1024,896]{1,0:T(8,128)} fusion(bf16[896,1024]{1,0:T(8,128)(2,1)S(1)} %copy-done, bf16[1024,1024]{1,0:T(8,128)(2,1)} %gather_fusion, pred[1024]{0:T(1024)(128)(4,1)S(1)} %compare_and_fusion), kind=kOutput, calls=%fused_computation.3 | convolution fusion | flops 1880096768 | bytes 7603200 | tf_op jit(solution)/shard_map/dot_general | solution.py:14
  94.8 0.0 copy-start.2
  94.8 0.0 reduce-scatter.2.cloned.1.call-update
  94.8 0.9 copy-done.2
  95.7 0.2 stack.2
  95.9 0.0 copy-start.1
  95.9 66.0 %all_to_all.5 = bf16[16,64,896]{2,1,0:T(8,128)(2,1)S(1)} all-to-all(bf16[16,64,896]{2,1,0:T(8,128)(2,1)S(1)} %stack.2), channel_id=1, replica_groups=mesh['row'=16,'col'=32] {'row'}, dimensions={0} | all-to-all | bytes 3670016 | tf_op jit(solution)/shard_map/all_to_all | solution.py:23
  162.0 0.0 copy-done.1
  162.0 3.8 %convert_bitcast_fusion = bf16[896,1024]{0,1:T(8,128)(2,1)} fusion(bf16[1024,896]{1,0:T(8,128)(2,1)S(1)} %bitcast.5, bf16[1024,1024]{1,0:T(8,128)(2,1)S(1)} %copy-done.1, pred[1024]{0:T(1024)(128)(4,1)S(1)} %compare_and_fusion), kind=kOutput, calls=%fused_computation.2 | convolution fusion | flops 1881014272 | bytes 5768192 | tf_op jit(solution)/shard_map/dot_general | solution.py:8
  165.8 3.8 %copy.6 = bf16[896,1024]{1,0:T(8,128)(2,1)} copy(bf16[896,1024]{0,1:T(8,128)(2,1)} %convert_bitcast_fusion) | data formatting | bytes 3670016
  169.5 158.4 %reduce-scatter.2.cloned.1.call-done = f32[64,896]{1,0:T(8,128)} async-done(((f32[1024,896]{1,0:T(8,128)}), f32[64,896]{1,0:T(8,128)}) %reduce-scatter.2.cloned.1.call-update) | async-done | bytes 229392 | tf_op jit(solution)/shard_map/reduce_scatter | solution.py:27
  327.9 1.6 convert_element_type.11
Async XLA Ops:
  7.2 81.8 %copy-start = (bf16[896,1024]{1,0:T(8,128)(2,1)S(1)}, bf16[896,1024]{1,0:T(8,128)(2,1)}, u32[]{:S(2)}) copy-start(bf16[896,1024]{1,0:T(8,128)(2,1)} %param.6) | copy-start | bytes 5505028
  7.2 73.9 %all-gather.2.cloned.1.call-start = ((), (), s32[]{:S(2)}) async-start(), calls=%async_computation.2 | async-start | bytes 2162688 | tf_op jit(solution)/shard_map/all_gather | solution.py:20
  7.9 320.0 %reduce-scatter.2.cloned.1.call-start = ((), (), s32[]{:S(2)}) async-start(), calls=%async_computation.3 | async-start | bytes 3899392 | tf_op jit(solution)/shard_map/reduce_scatter | solution.py:27
  94.8 0.9 copy-start.2
  95.9 66.0 %copy-start.1 = (bf16[1024,1024]{1,0:T(8,128)(2,1)S(1)}, bf16[1024,1024]{1,0:T(8,128)(2,1)}, u32[]{:S(2)}) copy-start(bf16[1024,1024]{1,0:T(8,128)(2,1)} %gather_fusion) | copy-start | bytes 6291460
Sparse Core Ops, SparseCore 0:
  10.2 70.8 all-gather.1
  94.9 232.9 reduce-scatter.1
